TPU v7x, 32 devices: a whole 2x2x4 slice. The times are simulated.
32 devices in a mesh: row: 8 (over z, y), col: 4 (over x, core).
Axes of the slice: x: 2, y: 2, z: 4, core: 2. Of those that a mesh axis runs over, the one named last changes fastest.
Arguments:
- orbitals: bfloat16 [20480, 384], P(('row', 'col')), may hold values from -6 to 6
- coulomb: float32 [20480, 20480], P('row', 'col'), may hold values from -0.001953125 to 0.001953125
- interp: bfloat16 [4096, 20480], P('row', 'col'), may hold values from -0.0390625 to 0.0390625
Outputs:
- exchanged: bfloat16 [4096, 384], P(('row', 'col'))
All inputs are finite; a program needn't handle non-finite values.
Results may differ from a plain program's by a relative error of at most 0.018.
Values may be sent and summed in bfloat16 or wider, within the bound.
No kernel may reach another device: no remote copies, remote signals or barrier semaphores. Data moves between devices by JAX's collectives and lax.ppermute only.
A program may use at most 128 MiB of HBM per device.

v0:
```python
import jax
import jax.numpy as jnp
from jax import lax
from jax.sharding import PartitionSpec as P


def broadcast(value, axis, source):
    kept = jnp.where(lax.axis_index(axis) == source, value, 0).astype(value.dtype)
    return lax.psum(kept, axis)


def local(orbitals, coulomb, interp):
    near = lax.all_gather(orbitals, "col", axis=0, tiled=True)
    factor = lax.axis_size("row") // lax.axis_size("col")
    column = lax.axis_index("col")
    pieces = []
    for offset in range(factor):
        pieces.append(broadcast(near, "row", column * factor + offset))
    far = jnp.concatenate(pieces, 0)
    density = lax.dot_general(
        near, far, (((1,), (1,)), ((), ())), preferred_element_type=jnp.float32
    )
    weighted = (coulomb * density).astype(jnp.bfloat16)
    partial_sum = lax.dot_general(
        weighted, near, (((0,), (0,)), ((), ())), preferred_element_type=jnp.float32
    )
    share = lax.psum_scatter(partial_sum, "row", scatter_dimension=0, tiled=True).astype(
        jnp.bfloat16
    )
    contracted = lax.all_gather(share, "row", axis=0, tiled=True)
    terms = jnp.dot(interp, contracted, preferred_element_type=jnp.float32)
    return lax.psum_scatter(terms.astype(jnp.bfloat16), "col", scatter_dimension=0, tiled=True)


def solution(mesh):
    in_specs = (P(("row", "col"), None), P("row", "col"), P("row", "col"))
    out_specs = P(("row", "col"), None)
    return jax.shard_map(local, mesh=mesh, in_specs=in_specs, out_specs=out_specs, check_vma=False)
```

profile of v0, /device:TPU:0, one launch (start us, length us, event | category | flops | bytes accessed | tf_op | source)
XLA Modules:
  0.0 489.1 jit_solution(2194609867817106554)
XLA Ops:
  6.5 0.0 all-gather.3.cloned.1.call-start
  6.5 0.7 all-gather.3.cloned.1.call-update
  7.3 0.0 all-reduce.3.cloned.1.call-start
  7.3 26.2 %all-gather.3.cloned.1.call-done = bf16[2560,384]{1,0:T(8,128)(2,1)} async-done(((bf16[640,384]{1,0:T(8,128)(2,1)}), bf16[2560,384]{1,0:T(8,128)(2,1)}) %all-gather.3.cloned.1.call-update) | async-done | bytes 1966096 | tf_op jit(solution)/shard_map/all_gather | solution.py:13
  33.5 0.0 copy-start
  33.5 4.0 broadcast_select_fusion.1
  37.5 0.0 all-reduce.3.cloned.1.call-update
  37.5 0.0 reduce-scatter.5.cloned.1.call-start
  37.5 149.6 %all-reduce.3.cloned.1.call-done = (bf16[2560,384]{1,0:T(8,128)(2,1)}, bf16[2560,384]{1,0:T(8,128)(2,1)}) async-done(((bf16[2560,384]{1,0:T(8,128)(2,1)}, bf16[2560,384]{1,0:T(8,128)(2,1)}), (bf16[2560,384]{1,0:T(8,128)(2,1)}, bf16[2560,384]{1,0:T(8,128)(2,1)})) %all-reduce.3.cloned.1.call-update) | async-done | bytes 3932176 | tf_op jit(solution)/shard_map/psum | solution.py:9
  187.1 0.0 copy-done
  187.1 58.8 %fusion.1 = f32[5120,384]{1,0:T(8,128)} fusion(bf16[2560,384]{1,0:T(8,128)(2,1)S(1)} %copy-done, f32[2560,5120]{1,0:T(8,128)} %param.4, bf16[2560,384]{1,0:T(8,128)(2,1)} %get-tuple-element.5, bf16[2560,384]{1,0:T(8,128)(2,1)} %get-tuple-element.6), kind=kOutput, calls=%fused_computation.2 | convolution fusion | flops 20166737920 | bytes 66191360 | tf_op jit(solution)/shard_map/dot_general | solution.py:24
  245.9 0.0 reduce-scatter.5.cloned.1.call-update
  246.0 0.0 all-gather.5.cloned.1.call-start
  246.0 139.4 %reduce-scatter.5.cloned.1.call-done = f32[640,384]{1,0:T(8,128)} async-done(((f32[5120,384]{1,0:T(8,128)}), f32[640,384]{1,0:T(8,128)}) %reduce-scatter.5.cloned.1.call-update) | async-done | bytes 983056 | tf_op jit(solution)/shard_map/reduce_scatter | solution.py:27
  385.4 2.0 convert_element_type.16
  387.4 0.0 all-gather.5.cloned.1.call-update
  387.4 0.2 reduce-scatter.7.cloned.1.call-start
  387.7 68.5 %all-gather.5.cloned.1.call-done = bf16[5120,384]{1,0:T(8,128)(2,1)} async-done(((bf16[640,384]{1,0:T(8,128)(2,1)}), bf16[5120,384]{1,0:T(8,128)(2,1)}) %all-gather.5.cloned.1.call-update) | async-done | bytes 3932176 | tf_op jit(solution)/shard_map/all_gather | solution.py:30
  456.2 5.9 %fusion.8 = bf16[512,384]{0,1:T(8,128)(2,1)S(1)} fusion(bf16[5120,384]{1,0:T(8,128)(2,1)} %all-gather.5.cloned.1.call-done, bf16[512,5120]{1,0:T(8,128)(2,1)} %param.5), kind=kOutput, calls=%fused_computation.9 | convolution fusion | flops 2013462528 | bytes 9568256 | tf_op jit(solution)/shard_map/dot_general | solution.py:31
  462.1 0.9 copy.6
  463.0 0.0 reduce-scatter.7.cloned.1.call-update
  463.0 19.6 %reduce-scatter.7.cloned.1.call-done = bf16[128,384]{1,0:T(8,128)(2,1)} async-done(((bf16[512,384]{1,0:T(8,128)(2,1)}), bf16[128,384]{1,0:T(8,128)(2,1)}) %reduce-scatter.7.cloned.1.call-update) | async-done | bytes 98320 | tf_op jit(solution)/shard_map/reduce_scatter | solution.py:32
Async XLA Ops:
  6.5 26.9 %all-gather.3.cloned.1.call-start = ((), (), s32[]{:S(2)}) async-start(), calls=%async_computation.2 | async-start | bytes 2457600 | tf_op jit(solution)/shard_map/all_gather | solution.py:13
  7.3 179.8 %all-reduce.3.cloned.1.call-start = ((), (), s32[]{:S(2)}) async-start(), calls=%async_computation.6 | async-start | bytes 7864320 | tf_op jit(solution)/shard_map/psum | solution.py:9
  33.5 153.6 %copy-start = (bf16[2560,384]{1,0:T(8,128)(2,1)S(1)}, bf16[2560,384]{1,0:T(8,128)(2,1)}, u32[]{:S(2)}) copy-start(bf16[2560,384]{1,0:T(8,128)(2,1)} %all-gather.3.cloned.1.call-done) | copy-start | bytes 5898244
  37.5 347.9 %reduce-scatter.5.cloned.1.call-start = ((), (), s32[]{:S(2)}) async-start(), calls=%async_computation.3 | async-start | bytes 8847360 | tf_op jit(solution)/shard_map/reduce_scatter | solution.py:27
  246.0 210.2 %all-gather.5.cloned.1.call-start = ((), (), s32[]{:S(2)}) async-start(), calls=%async_computation.4 | async-start | bytes 4423680 | tf_op jit(solution)/shard_map/all_gather | solution.py:30
  387.4 95.2 %reduce-scatter.7.cloned.1.call-start = ((), (), s32[]{:S(2)}) async-start(), calls=%async_computation.5 | async-start | bytes 491520 | tf_op jit(solution)/shard_map/reduce_scatter | solution.py:32
Sparse Core Ops, SparseCore 0:
  8.9 24.5 all-gather.2
  37.6 149.4 all-reduce.2
  246.1 139.2 reduce-scatter.4
  387.5 68.5 all-gather.4
  463.2 19.4 reduce-scatter.6
where the time goes:
time: 489 us
  waiting for transfers between devices  404 us (83%)
  matrix products  64.8 us (13%)
  between operations  13.2 us (3%)
  other arithmetic  6.01 us (1%)
    psum x1, waiting for transfers between devices, broadcast(): return lax.psum(kept, axis)  150 us
    reduce_scatter x1, waiting for transfers between devices, local(): lax.psum_scatter(partial_sum, 'row', scatter_dimension=0, tiled=True)  139 us
    all_gather x1, waiting for transfers between devices, local(): contracted = lax.all_gather(share, 'row', axis=0, tiled=True)  68.5 us
    dot_general x1, matrix products, local(): lax.dot_general(weighted, near, (((0,), (0,)), ((), ())), preferred_eleme...  58.8 us
    all_gather x1, waiting for transfers between devices, local(): near = lax.all_gather(orbitals, 'col', axis=0, tiled=True)  26.2 us
    reduce_scatter x1, waiting for transfers between devices, local(): lax.psum_scatter(terms.astype(jnp.bfloat16), 'col', scatter_dimension=0,...  19.6 us
  transfers between devices with their start and end apart: 5, of which 5 were waited for; matrix products, arithmetic and copies ran while one was open for 0% of the time, Pallas kernels for 0%

commit v1 on v0

--- a/solution.py
+++ b/solution.py
@@ -27,7 +27,12 @@
     share = lax.psum_scatter(partial_sum, "row", scatter_dimension=0, tiled=True).astype(
         jnp.bfloat16
     )
-    contracted = lax.all_gather(share, "row", axis=0, tiled=True)
+    ring = [share]
+    for hop in range(7):
+        ring.append(lax.ppermute(ring[-1], "row", [(dev, (dev + 1) % 8) for dev in range(8)]))
+    contracted = jnp.roll(
+        jnp.concatenate(ring[::-1], axis=0), (lax.axis_index("row") + 1) * ring[0].shape[0], axis=0
+    )
     terms = jnp.dot(interp, contracted, preferred_element_type=jnp.float32)
     return lax.psum_scatter(terms.astype(jnp.bfloat16), "col", scatter_dimension=0, tiled=True)
 

time: 489 us -> 511 us (1.045)
  waiting for transfers between devices: 404 us -> 423 us
  local copies, waits for them, and re-layouts: 0.93 us -> 6.38 us
    ppermute x0 -> x7, waiting for transfers between devices: none -> 88.7 us  [local(): lax.ppermute(ring[-1], 'row', [(dev, (dev + 1) % 8) for dev in range(8)])]
    all_gather x1 -> x0, waiting for transfers between devices: 68.5 us -> none  [local(): contracted = lax.all_gather(share, 'row', axis=0, tiled=True)]
    unnamed x3 -> x23, local copies, waits for them, and re-layouts: 0.93 us -> 6.38 us
  transfers between devices with their start and end apart: 5 -> 11, of which waited for: 5 -> 11; matrix products, arithmetic and copies ran while one was open for 0% -> 0% of each run, Pallas kernels for 0% -> 0%
where the time goes in v1:
time: 511 us
  waiting for transfers between devices  423 us (83%)
  matrix products  61.1 us (12%)
  between operations  13.3 us (3%)
  local copies, waits for them, and re-layouts  6.38 us (1%)
  other arithmetic  5.48 us (1%)
    psum x1, waiting for transfers between devices, broadcast(): return lax.psum(kept, axis)  150 us
    reduce_scatter x1, waiting for transfers between devices, local(): lax.psum_scatter(partial_sum, 'row', scatter_dimension=0, tiled=True)  139 us
    ppermute x7, waiting for transfers between devices, local(): lax.ppermute(ring[-1], 'row', [(dev, (dev + 1) % 8) for dev in range(8)])  88.7 us
    dot_general x1, matrix products, local(): lax.dot_general(weighted, near, (((0,), (0,)), ((), ())), preferred_eleme...  58.8 us
    all_gather x1, waiting for transfers between devices, local(): near = lax.all_gather(orbitals, 'col', axis=0, tiled=True)  26.2 us
    reduce_scatter x1, waiting for transfers between devices, local(): lax.psum_scatter(terms.astype(jnp.bfloat16), 'col', scatter_dimension=0,...  18.2 us
  transfers between devices with their start and end apart: 11, of which 11 were waited for; matrix products, arithmetic and copies ran while one was open for 0% of the time, Pallas kernels for 0%

profile of v1, /device:TPU:0, one launch (start us, length us, event | category | flops | bytes accessed | tf_op | source)
XLA Modules:
  0.0 510.6 jit_solution(10982703738874280928)
XLA Ops:
  6.5 0.7 all-gather.2.cloned.1.call-update
  7.3 26.2 %all-gather.2.cloned.1.call-done = bf16[2560,384]{1,0:T(8,128)(2,1)} async-done(((bf16[640,384]{1,0:T(8,128)(2,1)}), bf16[2560,384]{1,0:T(8,128)(2,1)}) %all-gather.2.cloned.1.call-update) | async-done | bytes 1966096 | tf_op jit(solution)/shard_map/all_gather | solution.py:13
  33.5 4.0 broadcast_select_fusion.1
  37.5 149.6 %all-reduce.3.cloned.1.call-done = (bf16[2560,384]{1,0:T(8,128)(2,1)}, bf16[2560,384]{1,0:T(8,128)(2,1)}) async-done(((bf16[2560,384]{1,0:T(8,128)(2,1)}, bf16[2560,384]{1,0:T(8,128)(2,1)}), (bf16[2560,384]{1,0:T(8,128)(2,1)}, bf16[2560,384]{1,0:T(8,128)(2,1)})) %all-reduce.3.cloned.1.call-update) | async-done | bytes 3932176 | tf_op jit(solution)/shard_map/psum | solution.py:9
  187.1 58.8 %fusion.1 = f32[5120,384]{1,0:T(8,128)} fusion(bf16[2560,384]{1,0:T(8,128)(2,1)S(1)} %copy-done.1, f32[2560,5120]{1,0:T(8,128)} %param.4, bf16[2560,384]{1,0:T(8,128)(2,1)} %get-tuple-element.5, bf16[2560,384]{1,0:T(8,128)(2,1)} %get-tuple-element.6), kind=kOutput, calls=%fused_computation.2 | convolution fusion | flops 20166737920 | bytes 66191360 | tf_op jit(solution)/shard_map/dot_general | solution.py:24
  246.0 139.4 %reduce-scatter.5.cloned.1.call-done = f32[640,384]{1,0:T(8,128)} async-done(((f32[5120,384]{1,0:T(8,128)}), f32[640,384]{1,0:T(8,128)}) %reduce-scatter.5.cloned.1.call-update) | async-done | bytes 983056 | tf_op jit(solution)/shard_map/reduce_scatter | solution.py:27
  385.3 1.3 convert_element_type.16
  386.7 1.5 collective-permute-start
  388.2 13.1 %collective-permute-done = bf16[640,384]{1,0:T(8,128)(2,1)S(1)} collective-permute-done((bf16[640,384]{1,0:T(8,128)(2,1)S(1)}, bf16[640,384]{1,0:T(8,128)(2,1)S(1)}, u32[]{:S(2)}, u32[]{:S(2)}) %collective-permute-start) | collective-permute-done | bytes 491552 | tf_op jit(solution)/shard_map/ppermute | solution.py:32
  401.4 13.8 %collective-permute-done.1 = bf16[640,384]{1,0:T(8,128)(2,1)S(1)} collective-permute-done((bf16[640,384]{1,0:T(8,128)(2,1)S(1)}, bf16[640,384]{1,0:T(8,128)(2,1)S(1)}, u32[]{:S(2)}, u32[]{:S(2)}) %collective-permute-start.1) | collective-permute-done | bytes 491552 | tf_op jit(solution)/shard_map/ppermute | solution.py:32
  415.1 12.9 %collective-permute-done.2 = bf16[640,384]{1,0:T(8,128)(2,1)S(1)} collective-permute-done((bf16[640,384]{1,0:T(8,128)(2,1)S(1)}, bf16[640,384]{1,0:T(8,128)(2,1)S(1)}, u32[]{:S(2)}, u32[]{:S(2)}) %collective-permute-start.2) | collective-permute-done | bytes 491552 | tf_op jit(solution)/shard_map/ppermute | solution.py:32
  428.0 12.1 %collective-permute-done.3 = bf16[640,384]{1,0:T(8,128)(2,1)S(1)} collective-permute-done((bf16[640,384]{1,0:T(8,128)(2,1)S(1)}, bf16[640,384]{1,0:T(8,128)(2,1)S(1)}, u32[]{:S(2)}, u32[]{:S(2)}) %collective-permute-start.3) | collective-permute-done | bytes 491552 | tf_op jit(solution)/shard_map/ppermute | solution.py:32
  440.1 12.0 %collective-permute-done.4 = bf16[640,384]{1,0:T(8,128)(2,1)S(1)} collective-permute-done((bf16[640,384]{1,0:T(8,128)(2,1)S(1)}, bf16[640,384]{1,0:T(8,128)(2,1)S(1)}, u32[]{:S(2)}, u32[]{:S(2)}) %collective-permute-start.4) | collective-permute-done | bytes 491552 | tf_op jit(solution)/shard_map/ppermute | solution.py:32
  452.1 12.9 %collective-permute-done.5 = bf16[640,384]{1,0:T(8,128)(2,1)} collective-permute-done((bf16[640,384]{1,0:T(8,128)(2,1)S(1)}, bf16[640,384]{1,0:T(8,128)(2,1)}, u32[]{:S(2)}, u32[]{:S(2)}) %collective-permute-start.5) | collective-permute-done | bytes 491552 | tf_op jit(solution)/shard_map/ppermute | solution.py:32
  465.0 11.8 %collective-permute-done.6 = bf16[640,384]{1,0:T(8,128)(2,1)} collective-permute-done((bf16[640,384]{1,0:T(8,128)(2,1)}, bf16[640,384]{1,0:T(8,128)(2,1)}, u32[]{:S(2)}, u32[]{:S(2)}) %collective-permute-start.6) | collective-permute-done | bytes 491552 | tf_op jit(solution)/shard_map/ppermute | solution.py:32
  476.9 1.1 constant_dynamic-update-slice_fusion.15
  478.0 1.3 constant_dynamic-update-slice_fusion.14
  479.2 0.1 constant_dynamic-update-slice_fusion.13
  479.3 0.1 constant_dynamic-update-slice_fusion.12
  479.4 0.1 constant_dynamic-update-slice_fusion.11
  479.5 0.1 constant_dynamic-update-slice_fusion.10
  479.7 0.1 constant_dynamic-update-slice_fusion.8
  479.8 1.2 constant_dynamic-update-slice_fusion.7
  481.0 1.1 constant_dynamic-update-slice_fusion.6
  482.1 0.1 constant_dynamic-update-slice_fusion.5
  482.2 0.1 constant_dynamic-update-slice_fusion.4
  482.3 0.1 constant_dynamic-update-slice_fusion.3
  482.5 0.1 constant_dynamic-update-slice_fusion.1
  482.5 0.1 constant_dynamic-update-slice_fusion
  482.7 2.3 fusion.13
  484.9 0.9 copy.6
  485.9 18.2 %reduce-scatter.7.cloned.1.call-done = bf16[128,384]{1,0:T(8,128)(2,1)} async-done(((bf16[512,384]{1,0:T(8,128)(2,1)}), bf16[128,384]{1,0:T(8,128)(2,1)}) %reduce-scatter.7.cloned.1.call-update) | async-done | bytes 98320 | tf_op jit(solution)/shard_map/reduce_scatter | solution.py:37
  (24 shorter events, 0.4 us)
Async XLA Ops:
  6.5 26.9 %all-gather.2.cloned.1.call-start = ((), (), s32[]{:S(2)}) async-start(), calls=%async_computation.2 | async-start | bytes 2457600 | tf_op jit(solution)/shard_map/all_gather | solution.py:13
  7.3 179.8 %all-reduce.3.cloned.1.call-start = ((), (), s32[]{:S(2)}) async-start(), calls=%async_computation.5 | async-start | bytes 7864320 | tf_op jit(solution)/shard_map/psum | solution.py:9
  33.5 153.6 %copy-start.1 = (bf16[2560,384]{1,0:T(8,128)(2,1)S(1)}, bf16[2560,384]{1,0:T(8,128)(2,1)}, u32[]{:S(2)}) copy-start(bf16[2560,384]{1,0:T(8,128)(2,1)} %all-gather.2.cloned.1.call-done) | copy-start | bytes 5898244
  37.5 347.9 %reduce-scatter.5.cloned.1.call-start = ((), (), s32[]{:S(2)}) async-start(), calls=%async_computation.3 | async-start | bytes 8847360 | tf_op jit(solution)/shard_map/reduce_scatter | solution.py:27
  245.9 258.1 %reduce-scatter.7.cloned.1.call-start = ((), (), s32[]{:S(2)}) async-start(), calls=%async_computation.4 | async-start | bytes 491520 | tf_op jit(solution)/shard_map/reduce_scatter | solution.py:37
  385.3 94.4 %copy-start = (f32[640,384]{1,0:T(8,128)S(1)}, f32[640,384]{1,0:T(8,128)}, u32[]{:S(2)}) copy-start(f32[640,384]{1,0:T(8,128)} %reduce-scatter.5.cloned.1.call-done) | copy-start | bytes 2949124
  386.7 14.7 %collective-permute-start = (bf16[640,384]{1,0:T(8,128)(2,1)S(1)}, bf16[640,384]{1,0:T(8,128)(2,1)S(1)}, u32[]{:S(2)}, u32[]{:S(2)}) collective-permute-start(bf16[640,384]{1,0:T(8,128)(2,1)S(1)} %convert_element_type.16), channel_id=1, source_target_pairs={{0,4},{4,8},{8,12},{12,16},{16,20},{20,24},{24,28},{28,0},{1,5},{5... | collective-permute-start | bytes 1474568 | tf_op jit(solution)/shard_map/ppermute | solution.py:32
  401.3 13.8 %collective-permute-start.1 = (bf16[640,384]{1,0:T(8,128)(2,1)S(1)}, bf16[640,384]{1,0:T(8,128)(2,1)S(1)}, u32[]{:S(2)}, u32[]{:S(2)}) collective-permute-start(bf16[640,384]{1,0:T(8,128)(2,1)S(1)} %collective-permute-done), channel_id=1, source_target_pairs={{0,4},{4,8},{8,12},{12,16},{16,20},{20,24},{24,28},{28,0},{1,5},{5... | collective-permute-start | bytes 1474568 | tf_op jit(solution)/shard_map/ppermute | solution.py:32
  415.1 12.9 %collective-permute-start.2 = (bf16[640,384]{1,0:T(8,128)(2,1)S(1)}, bf16[640,384]{1,0:T(8,128)(2,1)S(1)}, u32[]{:S(2)}, u32[]{:S(2)}) collective-permute-start(bf16[640,384]{1,0:T(8,128)(2,1)S(1)} %collective-permute-done.1), channel_id=1, source_target_pairs={{0,4},{4,8},{8,12},{12,16},{16,20},{20,24},{24,28},{28,0},{1,5},{5... | collective-permute-start | bytes 1474568 | tf_op jit(solution)/shard_map/ppermute | solution.py:32
  428.0 12.1 %collective-permute-start.3 = (bf16[640,384]{1,0:T(8,128)(2,1)S(1)}, bf16[640,384]{1,0:T(8,128)(2,1)S(1)}, u32[]{:S(2)}, u32[]{:S(2)}) collective-permute-start(bf16[640,384]{1,0:T(8,128)(2,1)S(1)} %collective-permute-done.2), channel_id=1, source_target_pairs={{0,4},{4,8},{8,12},{12,16},{16,20},{20,24},{24,28},{28,0},{1,5},{5... | collective-permute-start | bytes 1474568 | tf_op jit(solution)/shard_map/ppermute | solution.py:32
  440.1 12.0 %collective-permute-start.4 = (bf16[640,384]{1,0:T(8,128)(2,1)S(1)}, bf16[640,384]{1,0:T(8,128)(2,1)S(1)}, u32[]{:S(2)}, u32[]{:S(2)}) collective-permute-start(bf16[640,384]{1,0:T(8,128)(2,1)S(1)} %collective-permute-done.3), channel_id=1, source_target_pairs={{0,4},{4,8},{8,12},{12,16},{16,20},{20,24},{24,28},{28,0},{1,5},{5... | collective-permute-start | bytes 1474568 | tf_op jit(solution)/shard_map/ppermute | solution.py:32
  452.1 12.9 %collective-permute-start.5 = (bf16[640,384]{1,0:T(8,128)(2,1)S(1)}, bf16[640,384]{1,0:T(8,128)(2,1)}, u32[]{:S(2)}, u32[]{:S(2)}) collective-permute-start(bf16[640,384]{1,0:T(8,128)(2,1)S(1)} %collective-permute-done.4), channel_id=1, source_target_pairs={{0,4},{4,8},{8,12},{12,16},{16,20},{20,24},{24,28},{28,0},{1,5},{5... | collective-permute-start | bytes 1474568 | tf_op jit(solution)/shard_map/ppermute | solution.py:32
  465.0 11.8 %collective-permute-start.6 = (bf16[640,384]{1,0:T(8,128)(2,1)}, bf16[640,384]{1,0:T(8,128)(2,1)}, u32[]{:S(2)}, u32[]{:S(2)}) collective-permute-start(bf16[640,384]{1,0:T(8,128)(2,1)} %collective-permute-done.5), channel_id=1, source_target_pairs={{0,4},{4,8},{8,12},{12,16},{16,20},{20,24},{24,28},{28,0},{1,5},{5... | collective-permute-start | bytes 1474568 | tf_op jit(solution)/shard_map/ppermute | solution.py:32
  478.0 4.7 slice-start
  479.8 2.9 slice-start.1
Sparse Core Ops, SparseCore 0:
  8.9 24.5 all-gather.1
  37.6 149.4 all-reduce.2
  246.0 139.2 reduce-scatter.4
  486.0 18.0 reduce-scatter.6

commit v2 on v0

--- a/solution.py
+++ b/solution.py
@@ -6,7 +6,7 @@
 
 def broadcast(value, axis, source):
     kept = jnp.where(lax.axis_index(axis) == source, value, 0).astype(value.dtype)
-    return lax.psum(kept, axis)
+    return jnp.sum(lax.all_gather(kept, axis), axis=0)
 
 
 def local(orbitals, coulomb, interp):

time: 489 us -> 779 us (1.59)
  waiting for transfers between devices: 404 us -> 673 us
  other arithmetic: 6.01 us -> 26.4 us
    all_gather x0 -> x2, waiting for transfers between devices: none -> 418 us  [broadcast(): return jnp.sum(lax.all_gather(kept, axis), axis=0)]
    psum x1 -> x0, waiting for transfers between devices: 150 us -> none  [broadcast(): return lax.psum(kept, axis)]
    reduce_sum x0 -> x2, other arithmetic: none -> 20.5 us  [broadcast(): return jnp.sum(lax.all_gather(kept, axis), axis=0)]
  transfers between devices with their start and end apart: 5 -> 6, of which waited for: 5 -> 6; matrix products, arithmetic and copies ran while one was open for 0% -> 1% of each run, Pallas kernels for 0% -> 0%
where the time goes in v2:
time: 779 us; the launch traced here: 778 us
  waiting for transfers between devices  673 us (86%)
  matrix products  64.7 us (8%)
  other arithmetic  26.4 us (3%)
  between operations  13.5 us (2%)
    all_gather x2, waiting for transfers between devices, broadcast(): return jnp.sum(lax.all_gather(kept, axis), axis=0)  418 us
    reduce_scatter x1, waiting for transfers between devices, local(): lax.psum_scatter(partial_sum, 'row', scatter_dimension=0, tiled=True)  138 us
    all_gather x1, waiting for transfers between devices, local(): contracted = lax.all_gather(share, 'row', axis=0, tiled=True)  68.4 us
    dot_general x1, matrix products, local(): lax.dot_general(weighted, near, (((0,), (0,)), ((), ())), preferred_eleme...  58.8 us
    all_gather x1, waiting for transfers between devices, local(): near = lax.all_gather(orbitals, 'col', axis=0, tiled=True)  26.2 us
    reduce_sum x2, other arithmetic, broadcast(): return jnp.sum(lax.all_gather(kept, axis), axis=0)  20.5 us
    reduce_scatter x1, waiting for transfers between devices, local(): lax.psum_scatter(terms.astype(jnp.bfloat16), 'col', scatter_dimension=0,...  19.6 us
  transfers between devices with their start and end apart: 6, of which 6 were waited for; matrix products, arithmetic and copies ran while one was open for 1% of the time, Pallas kernels for 0%

profile of v2, /device:TPU:0, one launch (start us, length us, event | category | flops | bytes accessed | tf_op | source)
XLA Modules:
  0.0 778.4 jit_solution(4564824747678490580)
XLA Ops:
  6.5 0.0 all-gather.7.cloned.1.call-start
  6.5 0.7 all-gather.7.cloned.1.call-update
  7.3 0.0 all-gather.11.cloned.1.call-start
  7.3 26.2 %all-gather.7.cloned.1.call-done = bf16[2560,384]{1,0:T(8,128)(2,1)} async-done(((bf16[640,384]{1,0:T(8,128)(2,1)}), bf16[2560,384]{1,0:T(8,128)(2,1)}) %all-gather.7.cloned.1.call-update) | async-done | bytes 1966096 | tf_op jit(solution)/shard_map/all_gather | solution.py:13
  33.5 3.8 broadcast_select_fusion.1
  37.3 0.0 all-gather.11.cloned.1.call-update
  37.3 0.0 all-gather.13.cloned.1.call-start
  37.4 0.7 all-gather.13.cloned.1.call-update
  38.1 0.0 reduce-scatter.5.cloned.1.call-start
  38.1 213.8 %all-gather.11.cloned.1.call-done = bf16[20480,384]{1,0:T(8,128)(2,1)} async-done(((bf16[2560,384]{1,0:T(8,128)(2,1)}), bf16[20480,384]{1,0:T(8,128)(2,1)}) %all-gather.11.cloned.1.call-update) | async-done | bytes 15728656 | tf_op jit(solution)/shard_map/all_gather | solution.py:9
  251.9 10.3 %reduce_sum.24 = bf16[2560,384]{1,0:T(8,128)(2,1)} reduce(bf16[8,2560,384]{2,1,0:T(8,128)(2,1)} %bitcast.15, bf16[]{:T(256)} %constant.17.clone.1), dimensions={0}, to_apply=%region_0.1 | reduce | flops 6881280 | bytes 17694722 | tf_op jit(solution)/shard_map/reduce_sum | solution.py:9
  262.3 204.5 %all-gather.13.cloned.1.call-done = bf16[20480,384]{1,0:T(8,128)(2,1)} async-done(((bf16[2560,384]{1,0:T(8,128)(2,1)}), bf16[20480,384]{1,0:T(8,128)(2,1)}) %all-gather.13.cloned.1.call-update) | async-done | bytes 15728656 | tf_op jit(solution)/shard_map/all_gather | solution.py:9
  466.8 0.0 copy-start
  466.8 10.2 %reduce_sum.25 = bf16[2560,384]{1,0:T(8,128)(2,1)} reduce(bf16[8,2560,384]{2,1,0:T(8,128)(2,1)} %bitcast.16, bf16[]{:T(256)} %constant.17.clone.1), dimensions={0}, to_apply=%region_1.2 | reduce | flops 6881280 | bytes 17694722 | tf_op jit(solution)/shard_map/reduce_sum | solution.py:9
  477.0 0.0 copy-done
  477.0 58.8 %fusion.1 = f32[5120,384]{1,0:T(8,128)} fusion(bf16[2560,384]{1,0:T(8,128)(2,1)S(1)} %copy-done, f32[2560,5120]{1,0:T(8,128)} %param.4, bf16[2560,384]{1,0:T(8,128)(2,1)} %reduce_sum.25, bf16[2560,384]{1,0:T(8,128)(2,1)} %reduce_sum.24), kind=kOutput, calls=%fused_computation.2 | convolution fusion | flops 20166737920 | bytes 66191360 | tf_op jit(solution)/shard_map/dot_general | solution.py:24
  535.8 0.0 reduce-scatter.5.cloned.1.call-update
  535.8 0.0 all-gather.9.cloned.1.call-start
  535.9 138.5 %reduce-scatter.5.cloned.1.call-done = f32[640,384]{1,0:T(8,128)} async-done(((f32[5120,384]{1,0:T(8,128)}), f32[640,384]{1,0:T(8,128)}) %reduce-scatter.5.cloned.1.call-update) | async-done | bytes 983056 | tf_op jit(solution)/shard_map/reduce_scatter | solution.py:27
  674.4 2.0 convert_element_type.20
  676.4 0.0 all-gather.9.cloned.1.call-update
  676.4 0.3 reduce-scatter.7.cloned.1.call-start
  676.7 68.4 %all-gather.9.cloned.1.call-done = bf16[5120,384]{1,0:T(8,128)(2,1)} async-done(((bf16[640,384]{1,0:T(8,128)(2,1)}), bf16[5120,384]{1,0:T(8,128)(2,1)}) %all-gather.9.cloned.1.call-update) | async-done | bytes 3932176 | tf_op jit(solution)/shard_map/all_gather | solution.py:30
  745.2 5.9 fusion.8
  751.1 0.9 copy.6
  752.0 0.0 reduce-scatter.7.cloned.1.call-update
  752.0 19.6 %reduce-scatter.7.cloned.1.call-done = bf16[128,384]{1,0:T(8,128)(2,1)} async-done(((bf16[512,384]{1,0:T(8,128)(2,1)}), bf16[128,384]{1,0:T(8,128)(2,1)}) %reduce-scatter.7.cloned.1.call-update) | async-done | bytes 98320 | tf_op jit(solution)/shard_map/reduce_scatter | solution.py:32
Async XLA Ops:
  6.5 26.9 %all-gather.7.cloned.1.call-start = ((), (), s32[]{:S(2)}) async-start(), calls=%async_computation.2 | async-start | bytes 2457600 | tf_op jit(solution)/shard_map/all_gather | solution.py:13
  7.3 244.7 %all-gather.11.cloned.1.call-start = ((), (), s32[]{:S(2)}) async-start(), calls=%async_computation.5 | async-start | bytes 17694720 | tf_op jit(solution)/shard_map/all_gather | solution.py:9
  37.3 429.5 %all-gather.13.cloned.1.call-start = ((), (), s32[]{:S(2)}) async-start(), calls=%async_computation.6 | async-start | bytes 17694720 | tf_op jit(solution)/shard_map/all_gather | solution.py:9
  38.1 636.3 %reduce-scatter.5.cloned.1.call-start = ((), (), s32[]{:S(2)}) async-start(), calls=%async_computation.3 | async-start | bytes 8847360 | tf_op jit(solution)/shard_map/reduce_scatter | solution.py:27
  466.8 10.2 %copy-start = (bf16[2560,384]{1,0:T(8,128)(2,1)S(1)}, bf16[2560,384]{1,0:T(8,128)(2,1)}, u32[]{:S(2)}) copy-start(bf16[2560,384]{1,0:T(8,128)(2,1)} %all-gather.7.cloned.1.call-done) | copy-start | bytes 5898244
  535.8 209.3 %all-gather.9.cloned.1.call-start = ((), (), s32[]{:S(2)}) async-start(), calls=%async_computation.4 | async-start | bytes 4423680 | tf_op jit(solution)/shard_map/all_gather | solution.py:30
  676.4 95.2 %reduce-scatter.7.cloned.1.call-start = ((), (), s32[]{:S(2)}) async-start(), calls=%async_computation.7 | async-start | bytes 491520 | tf_op jit(solution)/shard_map/reduce_scatter | solution.py:32
Sparse Core Ops, SparseCore 0:
  8.9 24.5 all-gather.6
  37.4 214.4 all-gather.10
  254.1 212.6 all-gather.12
  536.0 138.3 reduce-scatter.4
  676.6 68.5 all-gather.8
  752.1 19.4 reduce-scatter.6
